TPU v7x, 128 devices: a whole 4x4x4 slice. The times are simulated.
128 devices in a mesh: seq: 16 (over x, z), head: 8 (over y, core).
Axes of the slice: x: 4, y: 4, z: 4, core: 2. Of those that a mesh axis runs over, the one named last changes fastest.
Arguments:
- hidden: bfloat16 [16, 1536, 2560], P('seq', 'head'), may hold values from -6 to 6
- norm_gain: float32 [2560], replicated, may hold values from 0.1 to 1.9
- w_qkv: bfloat16 [2560, 3840], P('seq'), may hold values from -0.15625 to 0.15625
- w_out: bfloat16 [2560, 2560], P(None, 'seq'), may hold values from -0.625 to 0.625
- kv_cache: bfloat16 [16, 4096, 1280], P('seq', None, 'head'), as said below
- new_len: int32 [16], replicated, may hold values from 1 to 1536, 12288 in all
- prefix_len: int32 [16], replicated, may hold values from 0 to 12287
Outputs:
- attn_out: bfloat16 [16, 1536, 2560], P('seq', 'head')
- kv_written: bfloat16 [16, 1536, 1280], P('seq', None, 'head')
Inputs may be any that keep to these rules, and one draw needn't show every extreme that they name: `new_len`: the lengths sum to 12288 and the largest is 1536. `kv_cache`: keys are stored already rotated to their positions.
All inputs are finite; a program needn't handle non-finite values.
Results may differ from a plain program's by a relative error of at most 0.008.
The roundings to bfloat16 on the way count: a program that leaves them out, or rounds other values in their place, can miss the bound.
Values may be sent and summed in bfloat16 or wider, within the bound.
A program may use at most 128 MiB of HBM per device.

v0:
```python
import math

import jax
import jax.numpy as jnp
from jax import lax
from jax.sharding import PartitionSpec as P

HEAD_DIM = 80
WINDOW = 4096
QBLOCK = 128
GROUP = 4


def normalize(hidden, norm_gain):
    values = hidden.astype(jnp.float32)
    meansq = jnp.mean(values * values, axis=-1, keepdims=True)
    return (values * lax.rsqrt(meansq + 1e-05) * norm_gain).astype(jnp.bfloat16)


def rotate(values, position):
    halfway = values.shape[-1] // 2
    frequency = jnp.exp(
        jnp.arange(halfway, dtype=jnp.float32) * (-2.0 * math.log(10000.0) / values.shape[-1])
    )
    angles = position.astype(jnp.float32)[..., None] * frequency
    cosine = jnp.cos(angles)
    sine_part = jnp.sin(angles)
    leading = values[..., :halfway]
    trailing = values[..., halfway:]
    return jnp.concatenate(
        [leading * cosine - trailing * sine_part, trailing * cosine + leading * sine_part], axis=-1
    )


def rotate_pack(projected, position):
    queries = rotate(projected[:, :, :GROUP, :], position[:, None, None]).astype(jnp.bfloat16)
    keys_new = rotate(projected[:, :, GROUP, :], position[:, None]).astype(jnp.bfloat16)
    values_new = projected[:, :, GROUP + 1, :].astype(jnp.bfloat16)
    return jnp.concatenate([queries, keys_new[:, :, None, :], values_new[:, :, None, :]], axis=2)


def shards(hidden, norm_gain, w_qkv, w_out, kv_cache, new_len, prefix_len):
    seq_index = lax.axis_index("seq")
    head_index = lax.axis_index("head")
    head_count = lax.axis_size("head")
    unused_lead, per_slice, width = hidden.shape
    total_cols = w_qkv.shape[1]
    all_groups = total_cols // ((GROUP + 2) * HEAD_DIM)
    groups = all_groups // head_count
    head_cols = groups * GROUP * HEAD_DIM
    new_total = head_count * per_slice
    score_scale = 1.0 / math.sqrt(HEAD_DIM)
    picker = jnp.arange(new_len.shape[0], dtype=jnp.int32) == seq_index
    length = jnp.sum(jnp.where(picker, new_len, 0))
    prefix = jnp.sum(jnp.where(picker, prefix_len, 0))
    normed = normalize(hidden.reshape(per_slice, width), norm_gain)
    projected = jnp.dot(
        normed, lax.all_gather(w_qkv, "seq", axis=0, tiled=True), preferred_element_type=jnp.float32
    )
    position = prefix + head_index * per_slice + jnp.arange(per_slice, dtype=jnp.int32)
    packed = rotate_pack(projected.reshape(per_slice, all_groups, GROUP + 2, HEAD_DIM), position)
    packed = packed.reshape(per_slice, all_groups, (GROUP + 2) * HEAD_DIM)
    received = lax.all_to_all(packed, "head", split_axis=1, concat_axis=0, tiled=True)
    received = received.reshape(new_total, groups, GROUP + 2, HEAD_DIM)
    row_index = jnp.arange(new_total, dtype=jnp.int32)
    live_rows = row_index < length
    written = received[:, :, GROUP:, :]
    written = jnp.where(live_rows[:, None, None, None], written, jnp.zeros_like(written))
    kv_written = written.reshape(1, new_total, groups * 2 * HEAD_DIM)
    cached = kv_cache.reshape(WINDOW, groups, 2, HEAD_DIM)
    keys_all = jnp.concatenate([cached[:, :, 0], received[:, :, GROUP]], axis=0)
    values_all = jnp.concatenate([cached[:, :, 1], received[:, :, GROUP + 1]], axis=0)
    queries_own = received[:, :, :GROUP]
    key_span = WINDOW + QBLOCK
    blocks = new_total // QBLOCK

    def attend(block_number):
        block_start = block_number * QBLOCK
        block_queries = lax.dynamic_slice_in_dim(queries_own, block_start, QBLOCK, 0)
        block_keys = lax.dynamic_slice_in_dim(keys_all, block_start, key_span, 0)
        block_values = lax.dynamic_slice_in_dim(values_all, block_start, key_span, 0)
        scores = (
            jnp.einsum(
                "qhgd,khd->hgqk", block_queries, block_keys, preferred_element_type=jnp.float32
            )
            * score_scale
        )
        query_index = block_start + jnp.arange(QBLOCK, dtype=jnp.int32)
        key_slot = block_start + jnp.arange(key_span, dtype=jnp.int32)
        allowed = (
            (key_slot[None, :] > query_index[:, None])
            & (key_slot[None, :] <= query_index[:, None] + WINDOW)
            & (key_slot[None, :] >= WINDOW - prefix)
        )
        scores = jnp.where(allowed[None, None], scores, -jnp.inf)
        row_max = jnp.max(scores, axis=-1, keepdims=True)
        weights = jnp.exp(scores - row_max)
        probabilities = (weights / jnp.sum(weights, axis=-1, keepdims=True)).astype(jnp.bfloat16)
        attended = jnp.einsum(
            "hgqk,khd->qhgd", probabilities, block_values, preferred_element_type=jnp.float32
        )
        attended = jnp.where((query_index < length)[:, None, None, None], attended, 0.0)
        return attended.astype(jnp.bfloat16).reshape(QBLOCK, head_cols)

    def run_block(block_number):
        return attend(block_number)

    attended_all = lax.map(run_block, jnp.arange(blocks, dtype=jnp.int32)).reshape(
        new_total, head_cols
    )
    outgoing = attended_all.reshape(head_count, per_slice, 1, head_cols)
    returned = lax.all_to_all(outgoing, "head", split_axis=0, concat_axis=2, tiled=True)
    returned = returned.reshape(per_slice, head_count * head_cols)
    output = jnp.dot(
        returned,
        lax.all_gather(w_out, "seq", axis=1, tiled=True),
        preferred_element_type=jnp.float32,
    )
    return (output.astype(jnp.bfloat16).reshape(1, per_slice, width), kv_written)


def solution(mesh):
    placed = (
        P("seq", "head", None),
        P(),
        P("seq", None),
        P(None, "seq"),
        P("seq", None, "head"),
        P(),
        P(),
    )
    return jax.shard_map(
        shards,
        mesh=mesh,
        in_specs=placed,
        out_specs=(P("seq", "head", None), P("seq", None, "head")),
        check_vma=False,
    )
```

profile of v0, /device:TPU:1, one launch (start us, length us, event | category | flops | bytes accessed | tf_op | source)
XLA Modules:
  0.0 375.2 jit_solution(16028717156881137376)
XLA Ops:
  7.9 1.4 fusion.31
  10.0 1.5 fusion.21
  11.7 127.9 %all-gather.3.cloned.1.call-done = bf16[2560,3840]{1,0:T(8,128)(2,1)} async-done(((bf16[160,3840]{1,0:T(8,128)(2,1)}), bf16[2560,3840]{1,0:T(8,128)(2,1)}) %all-gather.3.cloned.1.call-update) | async-done | bytes 19660816 | tf_op jit(solution)/shard_map/all_gather | solution.py:58
  139.6 24.0 %copy.20 = bf16[3840,2560]{1,0:T(8,128)(2,1)} copy(bf16[3840,2560]{0,1:T(8,128)(2,1)} %bitcast.102) | data formatting | bytes 39321600 | tf_op jit(solution)/shard_map/dot_general | solution.py:57
  163.6 9.9 %fusion.25 = f32[192,8,6,80]{0,3,2,1:T(8,128)S(1)} fusion(bf16[8,6,80,2560]{3,2,1,0:T(8,128)(2,1)} %bitcast.103, bf16[1,192,2560]{2,1,0:T(8,128)(2,1)S(1)} %copy-done.4, f32[2560]{0:T(1024)S(1)} %copy-done.7, f32[192]{0:T(256)S(1)} %add_rsqrt_fusion), kind=kOutput, calls=%fused_computation.35 | convolution fusion | flops 3776839680 | bytes 23603968 | tf_op jit(solution)/shard_map/dot_general | solution.py:57
  174.5 2.8 copy.22
  177.2 5.1 %all-to-all-start = ((bf16[192,8,480]{2,0,1:T(8,128)(2,1)}), bf16[192,8,480]{2,0,1:T(8,128)(2,1)S(1)}, u32[]{:S(2)}, u32[]{:S(2)}) async-start(bf16[192,8,480]{2,0,1:T(8,128)(2,1)} %copy.22), calls=%async_computation | async-start | bytes 3145728 | tf_op jit(solution)/shard_map/all_to_all | solution.py:63
  183.8 1.1 slice_bitcast_fusion
  184.9 18.1 %all-to-all-done = bf16[192,8,480]{2,0,1:T(8,128)(2,1)S(1)} async-done(((bf16[192,8,480]{2,0,1:T(8,128)(2,1)}), bf16[192,8,480]{2,0,1:T(8,128)(2,1)S(1)}, u32[]{:S(2)}, u32[]{:S(2)}) %all-to-all-start) | async-done | bytes 1474592 | tf_op jit(solution)/shard_map/all_to_all | solution.py:63
  203.0 1.2 copy-done
  204.2 3.5 copy.23
  207.7 1.6 reshape.375
  212.4 122.0 %while.12 = (s32[]{:T(128)}, bf16[12,128,320]{1,2,0:T(8,128)(2,1)S(1)}, s32[12]{0:T(128)S(1)}, s32[]{:T(128)}, bf16[5632,1,80]{0,2,1:T(8,128)(2,1)}, /*index=5*/...) while((s32[]{:T(128)}, ...), condition=%wide.region_6.7_spmd, body=%wide.region_3.6_spmd.sunk | while | flops 711618432 | bytes 32372892 | solution.py:108
  214.4 3.0 and_and_fusion.2
  217.4 2.4 fusion.44
  219.8 1.1 fusion.45
  221.0 1.6 fusion.46
  224.5 3.0 and_and_fusion.2
  227.5 2.4 fusion.44
  229.9 1.1 fusion.45
  231.1 1.6 fusion.46
  234.7 3.0 and_and_fusion.2
  237.7 2.4 fusion.44
  240.1 1.1 fusion.45
  241.3 1.6 fusion.46
  244.9 3.0 and_and_fusion.2
  247.9 2.5 fusion.44
  250.4 1.1 fusion.45
  251.5 1.6 fusion.46
  255.1 3.0 and_and_fusion.2
  258.1 2.4 fusion.44
  260.5 1.1 fusion.45
  261.7 1.6 fusion.46
  265.3 3.0 and_and_fusion.2
  268.3 2.4 fusion.44
  270.7 1.1 fusion.45
  271.9 1.6 fusion.46
  275.5 3.0 and_and_fusion.2
  278.4 2.4 fusion.44
  280.9 1.1 fusion.45
  282.0 1.6 fusion.46
  285.6 3.0 and_and_fusion.2
  288.6 2.4 fusion.44
  291.0 1.1 fusion.45
  292.2 1.6 fusion.46
  295.8 3.0 and_and_fusion.2
  298.8 2.4 fusion.44
  301.2 1.1 fusion.45
  302.4 1.6 fusion.46
  305.9 3.0 and_and_fusion.2
  308.9 2.4 fusion.44
  311.4 1.1 fusion.45
  312.5 1.6 fusion.46
  316.1 3.0 and_and_fusion.2
  319.1 2.4 fusion.44
  322.7 1.6 fusion.46
  326.3 3.0 and_and_fusion.2
  329.3 2.4 fusion.44
  331.7 1.1 fusion.45
  332.9 1.6 fusion.46
  334.5 1.4 copy.24
  335.9 4.3 %all-to-all-start.1 = ((bf16[8,192,1,320]{3,1,2,0:T(8,128)(2,1)}), bf16[8,192,1,320]{3,1,2,0:T(8,128)(2,1)S(1)}, u32[]{:S(2)}, u32[]{:S(2)}) async-start(bf16[8,192,1,320]{3,1,2,0:T(8,128)(2,1)} %bitcast.107), calls=%async_computation.1 | async-start | bytes 2359296 | tf_op jit(solution)/shard_map/all_to_all | solution.py:112
  341.7 15.1 %all-to-all-done.1 = bf16[8,192,1,320]{3,1,2,0:T(8,128)(2,1)S(1)} async-done(((bf16[8,192,1,320]{3,1,2,0:T(8,128)(2,1)}), bf16[8,192,1,320]{3,1,2,0:T(8,128)(2,1)S(1)}, u32[]{:S(2)}, u32[]{:S(2)}) %all-to-all-start.1) | async-done | bytes 983072 | tf_op jit(solution)/shard_map/all_to_all | solution.py:112
  358.3 10.0 %fusion.20 = bf16[1,192,2560]{2,1,0:T(8,128)(2,1)} fusion(bf16[192,2560]{1,0:T(8,128)(2,1)S(1)} %reshape.376, bf16[2560,2560]{0,1:T(8,128)(2,1)} %all-gather.5.cloned.1.call-done), kind=kOutput, calls=%fused_computation.25 | convolution fusion | flops 2517073920 | bytes 15073280 | tf_op jit(solution)/shard_map/dot_general | solution.py:114
  (135 shorter events, 25.4 us)
Async XLA Ops:
  7.2 132.4 %all-gather.3.cloned.1.call-start = ((), (), s32[]{:S(2)}) async-start(), calls=%async_computation.2 | async-start | bytes 20889600 | tf_op jit(solution)/shard_map/all_gather | solution.py:58
  139.6 24.0 %copy-start.4 = (bf16[1,192,2560]{2,1,0:T(8,128)(2,1)S(1)}, bf16[1,192,2560]{2,1,0:T(8,128)(2,1)}, u32[]{:S(2)}) copy-start(bf16[1,192,2560]{2,1,0:T(8,128)(2,1)} %param.9) | copy-start | bytes 2949124
  139.6 24.0 %copy-start.7 = (f32[2560]{0:T(1024)S(1)}, f32[2560]{0:T(1024)}, u32[]{:S(2)}) copy-start(f32[2560]{0:T(1024)} %param.10) | copy-start | bytes 30724
  177.2 6.5 %copy-start.3 = (bf16[1,4096,160]{1,2,0:T(8,128)(2,1)S(1)}, bf16[1,4096,160]{1,2,0:T(8,128)(2,1)}, u32[]{:S(2)}) copy-start(bf16[1,4096,160]{1,2,0:T(8,128)(2,1)} %param.13) | copy-start | bytes 3932164
  177.2 25.8 %all-to-all-start = ((bf16[192,8,480]{2,0,1:T(8,128)(2,1)}), bf16[192,8,480]{2,0,1:T(8,128)(2,1)S(1)}, u32[]{:S(2)}, u32[]{:S(2)}) async-start(bf16[192,8,480]{2,0,1:T(8,128)(2,1)} %copy.22), calls=%async_computation | async-start | bytes 3145728 | tf_op jit(solution)/shard_map/all_to_all | solution.py:63
  182.3 176.0 %all-gather.5.cloned.1.call-start = ((), (), s32[]{:S(2)}) async-start(), calls=%async_computation.3 | async-start | bytes 13926400 | tf_op jit(solution)/shard_map/all_gather | solution.py:116
  203.0 1.2 copy-start
  209.4 1.1 copy-start.2
  209.4 2.1 copy-start.1
  209.5 2.9 copy-start.5
  219.8 1.2 copy-start.6
  229.9 1.2 copy-start.6
  240.1 1.2 copy-start.6
  250.3 1.2 copy-start.6
  260.5 1.2 copy-start.6
  270.7 1.2 copy-start.6
  280.9 1.2 copy-start.6
  291.0 1.2 copy-start.6
  301.2 1.2 copy-start.6
  311.3 1.2 copy-start.6
  321.5 1.2 copy-start.6
  331.7 1.2 copy-start.6
  335.9 20.9 %all-to-all-start.1 = ((bf16[8,192,1,320]{3,1,2,0:T(8,128)(2,1)}), bf16[8,192,1,320]{3,1,2,0:T(8,128)(2,1)S(1)}, u32[]{:S(2)}, u32[]{:S(2)}) async-start(bf16[8,192,1,320]{3,1,2,0:T(8,128)(2,1)} %bitcast.107), calls=%async_computation.1 | async-start | bytes 2359296 | tf_op jit(solution)/shard_map/all_to_all | solution.py:112
Sparse Core Ops, SparseCore 0:
  10.2 129.3 all-gather.2
  185.3 92.1 all-gather.4
where the time goes:
time: 377 us; the launch traced here: 375 us
  waiting for transfers between devices  162 us (43%)
  matrix products  68.3 us (18%)
  other arithmetic  64.6 us (17%)
  local copies, waits for them, and re-layouts  45.9 us (12%)
  between operations  15.6 us (4%)
  starting transfers between devices  9.48 us (3%)
  loops' own time  8.78 us (2%)
    all_gather x1, waiting for transfers between devices, shards(): lax.all_gather(w_qkv, 'seq', axis=0, tiled=True)  128 us
    and x12, other arithmetic, attend(): (key_slot[None, :] > query_index[:, None]) & (key_slot[None, :] <= query_...  35.6 us
    dot_general x12, matrix products, attend(): jnp.einsum('qhgd,khd->hgqk', block_queries, block_keys, preferred_element...  29.2 us
    dot_general x1, local copies, waits for them, and re-layouts, shards(): jnp.dot(normed, lax.all_gather(w_qkv, 'seq', axis=0, tiled=True), preferr...  24 us
    dot_general x12, matrix products, attend(): jnp.einsum('hgqk,khd->qhgd', probabilities, block_values, preferred_eleme...  19.2 us
    all_to_all x1, waiting for transfers between devices, shards(): lax.all_to_all(packed, 'head', split_axis=1, concat_axis=0, tiled=True)  18.1 us
    all_to_all x1, waiting for transfers between devices, shards(): lax.all_to_all(outgoing, 'head', split_axis=0, concat_axis=2, tiled=True)  15.1 us
    reduce_sum x12, other arithmetic, attend(): jnp.sum(weights, axis=-1, keepdims=True)  13.6 us
  transfers between devices with their start and end apart: 4, of which 3 were waited for; matrix products, arithmetic and copies ran while one was open for 34% of the time, Pallas kernels for 0%

commit v1 on v0

v1 whole, which is shorter than its diff:
```python
import math

import jax
import jax.numpy as jnp
import numpy as np
from jax import lax
from jax.experimental import pallas as pl
from jax.experimental.pallas import tpu as pltpu
from jax.sharding import PartitionSpec as P

HEAD_DIM = 80
HALF = HEAD_DIM // 2
GROUP = 4
WINDOW = 4096
QBLOCK = 128
HIDE = -(2.0**127)
F32 = jnp.float32
BF16 = jnp.bfloat16
MESH = pl.DeviceIdType.MESH


def matmul(a, b):
    return lax.dot_general(a, b, (((1,), (0,)), ((), ())), preferred_element_type=F32)


def kernel(
    hidden, gain, w_mine, wo_mine, kv, cos_slot, sin_slot, cos_pre, sin_pre, new_len, prefix_len,
    out, written,
    rows, wq, wo, keys, vals, queries, state, maxes, ready, landed, finished,
    w_send, w_recv, o_send, o_recv, p_send, p_recv, y_send, y_recv, a_send, a_recv,
):
    s = lax.axis_index("seq")
    h = lax.axis_index("head")
    y, c = h // 2, h % 2
    own = hidden.shape[0]
    chip = 2 * own
    width = hidden.shape[1]
    piece = w_mine.shape[0]
    half_o = piece // 2
    length, prefix = new_len[s], prefix_len[s]
    x, z = s // 4, s % 4
    a, b = x + c * (z - x), z + c * (x - z)
    step_a, step_b = 4 - 3 * c, 1 + 3 * c

    def slot(da, db):
        return lax.rem(a + da + 4, 4) * step_a + lax.rem(b + db + 4, 4) * step_b

    def head_of(dy, core):
        return lax.rem(y + dy + 4, 4) * 2 + core

    def remote(src, dst, send, recv, seq_id, head_id):
        return pltpu.make_async_remote_copy(
            src_ref=src, dst_ref=dst, send_sem=send, recv_sem=recv,
            device_id={"seq": seq_id, "head": head_id}, device_id_type=MESH,
        )

    barrier = pltpu.get_barrier_semaphore()
    for da, db in ((1, 0), (-1, 0), (0, 1), (0, -1)):
        pl.semaphore_signal(barrier, inc=1, device_id={"seq": slot(da, db), "head": h}, device_id_type=MESH)
    for d in range(1, 8):
        pl.semaphore_signal(barrier, inc=1, device_id={"seq": s, "head": lax.rem(h + d, 8)}, device_id_type=MESH)
    pl.semaphore_wait(barrier, 11)

    turns = (0, -1, 1, 2)

    class Gather:
        def __init__(self, mine, whole, first, second, send, recv):
            self.mine, self.whole, self.first, self.second = mine, whole, first, second
            self.send, self.recv = send, recv

        def copy(self, m, src, dst, da, db):
            return remote(src, dst, self.send.at[m], self.recv.at[m], slot(da, db), h)

        def start_own(self):
            me = self.whole(slot(0, 0))
            self.copy(0, self.mine, me, 1, 0).start()
            self.copy(1, self.mine, me, -1, 0).start()
            self.copy(4, self.mine, me, 0, 1).start()
            self.copy(5, self.mine, me, 0, -1).start()

        def got(self, m, region):
            self.copy(m, region, region, 1, 0).wait_recv()

        def forward_b(self, q):
            region = self.whole(slot(turns[q], 0))
            self.copy(4 + 2 * q, region, region, 0, 1).start()
            self.copy(5 + 2 * q, region, region, 0, -1).start()

        def second_step(self):
            self.got(0, self.whole(slot(-1, 0)))
            self.got(1, self.whole(slot(1, 0)))
            ra, rb = self.first(slot(-1, 0)), self.second(slot(1, 0))
            self.copy(2, ra, ra, 1, 0).start()
            self.copy(3, rb, rb, -1, 0).start()
            self.forward_b(1)
            self.forward_b(2)

        def third_step(self):
            self.got(2, self.first(slot(2, 0)))
            self.got(3, self.second(slot(2, 0)))
            self.forward_b(3)

        def fourth_step(self):
            for q in range(4):
                self.got(4 + 2 * q, self.whole(slot(turns[q], -1)))
                self.got(5 + 2 * q, self.whole(slot(turns[q], 1)))
                ra, rb = self.first(slot(turns[q], -1)), self.second(slot(turns[q], 1))
                self.copy(12 + 2 * q, ra, ra, 0, 1).start()
                self.copy(13 + 2 * q, rb, rb, 0, -1).start()

        def last_step(self):
            for q in range(4):
                self.got(12 + 2 * q, self.first(slot(turns[q], 2)))
                self.got(13 + 2 * q, self.second(slot(turns[q], 2)))

        def drain(self):
            me = self.mine
            for m in (0, 1, 4, 5):
                self.copy(m, me, me, 1, 0).wait_send()
            for m in (2, 12, 14, 16, 18):
                r = self.first(slot(0, 0))
                self.copy(m, r, r, 1, 0).wait_send()
            for m in (3, 13, 15, 17, 19):
                r = self.second(slot(0, 0))
                self.copy(m, r, r, 1, 0).wait_send()
            for m in (6, 7, 8, 9, 10, 11):
                r = self.whole(slot(0, 0))
                self.copy(m, r, r, 1, 0).wait_send()

    def wq_rows(offset, count):
        return lambda sl: wq.at[pl.ds(pl.multiple_of(sl * piece + offset, 16), count)]

    gather_q = Gather(w_mine, wq_rows(0, piece), wq_rows(0, piece // 2), wq_rows(piece // 2, piece // 2), w_send, w_recv)

    def wo_part(core, lo, count):
        return lambda sl: wo.at[
            pl.ds(pl.multiple_of(sl * piece + core * half_o, 16), half_o), pl.ds(lo, count)
        ]

    gather_o = Gather(
        wo_mine.at[pl.ds(pl.multiple_of(c * half_o, 16), half_o)],
        wo_part(c, 0, width), wo_part(c, 0, width // 2), wo_part(c, width // 2, width // 2), o_send, o_recv,
    )

    def partner_copy(sl, core):
        region = wo_part(core, 0, width)(sl)
        return remote(region, region, p_send.at[sl], p_recv.at[sl], s, head_of(0, 1 - c))

    gather_q.start_own()

    def row_block(dy, core, offset=0, count=own):
        return rows.at[lax.rem(y + dy + 4, 4), pl.ds(pl.multiple_of(core * own + offset, 16), count)]

    def norm_rows(i, carry):
        values = hidden[pl.ds(pl.multiple_of(i * 32, 32), 32), :].astype(F32)
        meansq = jnp.mean(values * values, axis=-1, keepdims=True)
        normed = (values * lax.rsqrt(meansq + 1e-05) * gain[...]).astype(BF16)
        rows[y, pl.ds(pl.multiple_of(c * own + i * 32, 32), 32), :] = normed
        return carry

    lax.fori_loop(0, own // 32, norm_rows, 0)

    def y_copy(m, region, dy, core):
        return remote(region, region, y_send.at[m], y_recv.at[m], s, head_of(dy, core))

    y_copy(1, row_block(0, c), 1, c).start()
    y_copy(2, row_block(0, c), -1, c).start()
    y_copy(0, row_block(0, c), 0, 1 - c).start()

    wq[pl.ds(pl.multiple_of(s * piece, 16), piece), :] = w_mine[...]
    wo[pl.ds(pl.multiple_of(s * piece, 16), piece), :] = wo_mine[...]

    def prepare_cache(i, carry):
        at = pl.ds(pl.multiple_of(i * 256, 256), 256)
        block = kv[at, :].astype(F32)
        low = block[:, :128]
        lane = lax.broadcasted_iota(jnp.int32, (256, 128), 1)
        position = i * 256 + lax.broadcasted_iota(jnp.int32, (256, 128), 0)
        hidden_slot = (lane == HEAD_DIM) & (position < WINDOW - prefix)
        key = jnp.where(lane < HEAD_DIM, low, 0.0)
        keys[at, :128] = jnp.where(hidden_slot, HIDE, key).astype(BF16)
        keys[at, 128:] = key.astype(BF16)
        vals[:HEAD_DIM, at] = jnp.transpose(block)[HEAD_DIM:, :].astype(BF16)
        return carry

    lax.fori_loop(0, WINDOW // 256, prepare_cache, 0)
    total = vals.shape[1]
    one_row = (lax.broadcasted_iota(jnp.int32, (16, 512), 0) == 0).astype(F32).astype(BF16)
    for i in range(total // 512):
        vals[HEAD_DIM:, i * 512 : (i + 1) * 512] = one_row
    for k in range(4):
        for i in range(3):
            cols = slice(i * 512, (i + 1) * 512)
            queries[k, 80:96, cols] = one_row
            queries[k, 96:128, cols] = jnp.zeros((32, 512), BF16)
            queries[k, 208:256, cols] = jnp.zeros((48, 512), BF16)

    gather_q.second_step()
    gather_q.third_step()
    gather_q.fourth_step()
    gather_o.start_own()
    y_copy(0, row_block(0, 1 - c), 0, c).wait_recv()
    gather_q.last_step()

    scale = math.log2(math.e) / math.sqrt(HEAD_DIM)

    def project(yk):
        projected = jnp.transpose(matmul(rows[yk], wq[...]))
        tokens = pl.ds(pl.multiple_of(yk * chip, 128), chip)
        cn, sn = cos_slot[:, tokens], sin_slot[:, tokens]
        cp, sp = cos_pre[:, 0:1], sin_pre[:, 0:1]
        cosine, sine = cn * cp - sn * sp, sn * cp + cn * sp

        def rotate(at):
            lead, trail = projected[at : at + HALF], projected[at + HALF : at + HEAD_DIM]
            turned = jnp.concatenate([lead * cosine - trail * sine, trail * cosine + lead * sine], axis=0)
            return turned.astype(BF16).astype(F32)

        for g in range(GROUP):
            scaled = rotate(g * HEAD_DIM) * scale
            high = scaled.astype(BF16)
            low = (scaled - high.astype(F32)).astype(BF16)
            for j in range(3):
                cols = slice(j * 512 + g * 128, j * 512 + g * 128 + 128)
                toks = slice(j * 128, j * 128 + 128)
                queries[yk, 0:80, cols] = high[:, toks]
                queries[yk, 128:208, cols] = low[:, toks]
        key = rotate(GROUP * HEAD_DIM)
        value = projected[(GROUP + 1) * HEAD_DIM : (GROUP + 2) * HEAD_DIM].astype(BF16)
        slots = pl.ds(pl.multiple_of(WINDOW + yk * chip, 128), chip)
        vals[:HEAD_DIM, slots] = value
        pair = jnp.transpose(jnp.concatenate([key, value.astype(F32)], axis=0))
        index = yk * chip + lax.broadcasted_iota(jnp.int32, pair.shape, 0)
        written[tokens, :] = jnp.where(index < length, pair, 0.0).astype(BF16)
        lane = lax.broadcasted_iota(jnp.int32, (chip, 128), 1)
        clean = jnp.where(lane < HEAD_DIM, pair[:, :128], 0.0).astype(BF16)
        keys[slots, :128] = clean
        keys[slots, 128:] = clean

    def scores(start, count, block_queries):
        return matmul(keys[pl.ds(pl.multiple_of(start, 128), count), :], block_queries)

    def absorb(carry, sc, parts):
        peak, total_ = carry
        top = jnp.max(sc, axis=0, keepdims=True)
        if peak is not None:
            top = jnp.maximum(peak, top)
        weights = jnp.exp2(sc - top).astype(BF16)
        if peak is not None:
            total_ = total_ * jnp.exp2(peak - top)
        at = 0
        for start, count in parts:
            add = matmul(vals[:88, pl.ds(pl.multiple_of(start, 128), count)], weights[at : at + count])
            total_ = add if total_ is None else total_ + add
            at += count
        return top, total_

    common = 4 * chip
    chunk1 = 512

    def first_phase(yk):
        todo = [(j, common + i * chunk1) for j in range(3) for i in range((WINDOW - common) // chunk1)]
        per = len(todo) // 3

        def make(t):
            j, start = todo[t]
            return scores(start, chunk1, queries[yk, :, j * 512 : (j + 1) * 512])

        sc = make(0)
        carry = (None, None)
        for t in range(len(todo)):
            later = make(t + 1) if t + 1 < len(todo) else None
            j, start = todo[t]
            carry = absorb(carry, sc, [(start, chunk1)])
            if t % per == per - 1:
                cols = slice(j * 512, (j + 1) * 512)
                maxes[yk, :, cols] = carry[0]
                state[yk, :, cols] = carry[1]
                carry = (None, None)
            sc = later

    def second_phase(yk):
        base = yk * chip
        full = [
            jnp.where(yk + i < 3, base + (i + 1) * chip, WINDOW + (i - (3 - yk)) * chip) for i in range(3)
        ]

        def make(j, u):
            block_queries = queries[yk, :, j * 512 : (j + 1) * 512]
            if u < 3:
                return scores(full[u], chip, block_queries)
            lowest, upto = chip - j * 128, (j + 1) * 128
            row = lax.broadcasted_iota(jnp.int32, (128, 512), 0)
            col = lax.broadcasted_iota(jnp.int32, (128, 512), 1) & (QBLOCK - 1)
            low = scores(base + j * 128, lowest, block_queries)
            high = scores(WINDOW + base, upto, block_queries)
            parts = [jnp.where(row > col, low[:128], HIDE), low[128:], high[:-128], jnp.where(row <= col, high[-128:], HIDE)]
            return jnp.concatenate([p for p in parts if p.shape[0]], axis=0)

        units = [(j, u) for j in range(3) for u in range(4)]
        sc = make(*units[0])
        for t, (j, u) in enumerate(units):
            later = make(*units[t + 1]) if t + 1 < len(units) else None
            cols = slice(j * 512, (j + 1) * 512)
            if u == 0:
                carry = (maxes[yk, :, cols], state[yk, :, cols])
            if u < 3:
                parts = [(full[u], chip)]
            else:
                parts = [(base + j * 128, chip - j * 128), (WINDOW + base, (j + 1) * 128)]
            carry = absorb(carry, sc, parts)
            if u == 3:
                sums = carry[1]
                attended = sums[:HEAD_DIM] * (1.0 / sums[HEAD_DIM : HEAD_DIM + 1])
                token = base + j * 128 + (lax.broadcasted_iota(jnp.int32, (HEAD_DIM, 512), 1) & (QBLOCK - 1))
                attended = jnp.where(token < length, attended, 0.0).astype(BF16)
                for g in range(GROUP):
                    ready[yk, g * HEAD_DIM : (g + 1) * HEAD_DIM, j * 128 : (j + 1) * 128] = attended[:, g * 128 : (g + 1) * 128]
            sc = later

    def arrive(k):
        @pl.when(k == 1)
        def _():
            y_copy(1, row_block(-1, c), 0, c).wait_recv()
            y_copy(2, row_block(1, c), 0, c).wait_recv()
            r = row_block(-1, c, 0, own // 2)
            y_copy(5, r, 1, c).start()
            r = row_block(1, c, own // 2, own // 2)
            y_copy(6, r, -1, c).start()
            y_copy(3, row_block(-1, c), 0, 1 - c).start()
            y_copy(4, row_block(1, c), 0, 1 - c).start()
            gather_o.second_step()
            y_copy(3, row_block(-1, 1 - c), 0, c).wait_recv()

        @pl.when(k == 2)
        def _():
            gather_o.third_step()
            y_copy(4, row_block(1, 1 - c), 0, c).wait_recv()

        @pl.when(k == 3)
        def _():
            y_copy(5, row_block(2, c, 0, own // 2), 0, c).wait_recv()
            y_copy(6, row_block(2, c, own // 2, own // 2), 0, c).wait_recv()
            y_copy(7, row_block(2, c), 0, 1 - c).start()
            gather_o.fourth_step()
            for q in range(1, 4):
                partner_copy(slot(turns[q], 0), c).start()
            for q in range(4):
                partner_copy(slot(turns[q], -1), c).start()
                partner_copy(slot(turns[q], 1), c).start()
            y_copy(7, row_block(2, 1 - c), 0, c).wait_recv()

    def first_loop(k, carry):
        arrive(k)
        turn = jnp.where(k == 0, 0, jnp.where(k == 1, 3, k - 1))
        yk = lax.rem(y + turn, 4)
        project(yk)
        first_phase(yk)
        return carry

    lax.fori_loop(0, 4, first_loop, 0)

    def attended_copy(yk, core):
        src = ready.at[yk, :, pl.ds(pl.multiple_of(core * 128, 128), 256)]
        dst = landed.at[pl.ds(pl.multiple_of(h * GROUP * HEAD_DIM, 16), GROUP * HEAD_DIM)]
        return remote(src, dst, a_send.at[2 * yk + core], a_recv.at[h], s, 2 * yk + core)

    def second_loop(k, carry):
        turn = jnp.where(k == 0, 2, jnp.where(k == 1, 1, jnp.where(k == 2, 3, 0)))
        yk = lax.rem(y + turn, 4)

        @pl.when(k == 1)
        def _():
            gather_o.last_step()
            for q in range(4):
                partner_copy(slot(turns[q], 2), c).start()

        second_phase(yk)

        @pl.when(k < 3)
        def _():
            attended_copy(yk, 0).start()
            attended_copy(yk, 1).start()

        @pl.when(k == 3)
        def _():
            attended_copy(yk, 1 - c).start()

        return carry

    lax.fori_loop(0, 4, second_loop, 0)
    mine = pl.ds(pl.multiple_of(h * GROUP * HEAD_DIM, 16), GROUP * HEAD_DIM)
    landed[mine, :] = ready[y, :, pl.ds(pl.multiple_of(c * 128, 128), 256)]
    for d in range(1, 16):
        sl = lax.rem(s + d, 16)
        partner_copy(sl, 1 - c).wait_recv()
    for d in range(1, 8):
        src = lax.rem(h + d, 8)
        region = landed.at[pl.ds(pl.multiple_of(src * GROUP * HEAD_DIM, 16), GROUP * HEAD_DIM)]
        remote(region, region, a_send.at[0], a_recv.at[src], s, h).wait_recv()

    for i in range(width // 512):
        block = matmul(wo[i * 512 : (i + 1) * 512, :], landed[...])
        finished[:, i * 512 : (i + 1) * 512] = jnp.transpose(block)
    out[...] = finished[pl.ds(pl.multiple_of(c * (256 - own), 64), own), :].astype(BF16)

    gather_q.drain()
    gather_o.drain()
    for d in range(1, 16):
        partner_copy(lax.rem(s + d, 16), c).wait_send()
    for m in (0, 1, 2, 3, 4, 7):
        y_copy(m, row_block(0, c), 0, 1 - c).wait_send()
    for m in (5, 6):
        y_copy(m, row_block(0, c, 0, own // 2), 0, 1 - c).wait_send()
    for d in range(1, 8):
        dst = lax.rem(h + d, 8)
        region = landed.at[pl.ds(0, GROUP * HEAD_DIM)]
        remote(region, region, a_send.at[dst], a_recv.at[0], s, dst).wait_send()


def solution(mesh):
    def step(hidden, norm_gain, w_qkv, w_out, kv_cache, new_len, prefix_len):
        s, h = lax.axis_index("seq"), lax.axis_index("head")
        own, width = hidden.shape[1], hidden.shape[2]
        new_total = 8 * own
        wide = (GROUP + 2) * HEAD_DIM
        piece = w_qkv.shape[0]
        w_mine = lax.dynamic_slice(w_qkv, (0, h * wide), (piece, wide))
        wo_mine = w_out.T
        frequency = np.exp(np.arange(HALF, dtype=np.float64) * (-2.0 * math.log(10000.0) / HEAD_DIM))
        angles = frequency[:, None] * np.arange(new_total, dtype=np.float64)[None, :]
        cos_slot = jnp.asarray(np.cos(angles).astype(np.float32))
        sin_slot = jnp.asarray(np.sin(angles).astype(np.float32))
        prefix = lax.dynamic_index_in_dim(prefix_len, s, 0, keepdims=False).astype(F32)
        turn = prefix * jnp.asarray(frequency.astype(np.float32))
        cos_pre = jnp.broadcast_to(jnp.cos(turn)[:, None], (HALF, 128))
        sin_pre = jnp.broadcast_to(jnp.sin(turn)[:, None], (HALF, 128))
        chip = 2 * own
        dma = pltpu.SemaphoreType.DMA
        vmem = pl.BlockSpec(memory_space=pltpu.VMEM)
        smem = pl.BlockSpec(memory_space=pltpu.SMEM)
        attn_out, kv_written = pl.pallas_call(
            kernel,
            out_shape=(
                jax.ShapeDtypeStruct((own, width), BF16),
                jax.ShapeDtypeStruct((new_total, 2 * HEAD_DIM), BF16),
            ),
            in_specs=[vmem] * 9 + [smem] * 2,
            out_specs=(vmem, vmem),
            scratch_shapes=[
                pltpu.VMEM((4, chip, width), BF16),
                pltpu.VMEM((16 * piece, wide), BF16),
                pltpu.VMEM((16 * piece, width), BF16),
                pltpu.VMEM((WINDOW + new_total, 256), BF16),
                pltpu.VMEM((96, WINDOW + new_total), BF16),
                pltpu.VMEM((4, 256, 4 * chip), BF16),
                pltpu.VMEM((4, 88, 4 * chip), F32),
                pltpu.VMEM((4, 1, 4 * chip), F32),
                pltpu.VMEM((4, GROUP * HEAD_DIM, chip), BF16),
                pltpu.VMEM((8 * GROUP * HEAD_DIM, 256), BF16),
                pltpu.VMEM((256, width), F32),
                dma((20,)), dma((20,)), dma((20,)), dma((20,)), dma((16,)), dma((16,)),
                dma((8,)), dma((8,)), dma((8,)), dma((8,)),
            ],
            compiler_params=pltpu.CompilerParams(
                collective_id=0, has_side_effects=True, vmem_limit_bytes=62 * 1024 * 1024
            ),
        )(
            hidden.reshape(own, width), norm_gain.reshape(1, width), w_mine, wo_mine,
            kv_cache.reshape(WINDOW, 2 * HEAD_DIM), cos_slot, sin_slot, cos_pre, sin_pre, new_len, prefix_len,
        )
        return attn_out.reshape(1, own, width), kv_written.reshape(1, new_total, 2 * HEAD_DIM)

    return jax.shard_map(
        step,
        mesh=mesh,
        in_specs=(
            P("seq", "head", None), P(), P("seq", None), P(None, "seq"), P("seq", None, "head"), P(), P(),
        ),
        out_specs=(P("seq", "head", None), P("seq", None, "head")),
        check_vma=False,
    )
```

time: 377 us -> 101 us (0.27)
  waiting for transfers between devices: 162 us -> 0 us
  Pallas kernels: 0 us -> 87.4 us
  matrix products: 68.3 us -> 0 us
  other arithmetic: 64.6 us -> 0.7 us
  local copies, waits for them, and re-layouts: 45.9 us -> 11.7 us
  between operations: 15.6 us -> 1.32 us
  starting transfers between devices: 9.48 us -> 0 us
  loops' own time: 8.78 us -> 0 us
    all_gather x2 -> x0, waiting for transfers between devices: 128 us -> none  [the longest x1 128 us: shards(): lax.all_gather(w_qkv, 'seq', axis=0, tiled=True)]
    pallas_call x0 -> x1, Pallas kernels: none -> 87.4 us  [step(): pl.pallas_call(kernel, out_shape=(jax.ShapeDtypeStruct((own, width), BF16...]
    dot_general x26 -> x0, matrix products: 68.3 us -> none  [the longest x12 29.2 us: attend(): jnp.einsum('qhgd,khd->hgqk', block_queries, block_keys, preferred_element...]
    and x12 -> x0, other arithmetic: 35.6 us -> none  [attend(): (key_slot[None, :] > query_index[:, None]) & (key_slot[None, :] <= query_...]
    all_to_all x2 -> x0, waiting for transfers between devices: 33.2 us -> none  [the longest x1 18.1 us: shards(): lax.all_to_all(packed, 'head', split_axis=1, concat_axis=0, tiled=True)]
    dot_general x1 -> x0, local copies, waits for them, and re-layouts: 24 us -> none  [shards(): jnp.dot(normed, lax.all_gather(w_qkv, 'seq', axis=0, tiled=True), preferr...]
    reduce_sum x14 -> x0, other arithmetic: 16.5 us -> none  [the longest x12 13.6 us: attend(): jnp.sum(weights, axis=-1, keepdims=True)]
    all_to_all x2 -> x0, starting transfers between devices: 9.44 us -> none  [the longest x1 5.09 us: shards(): lax.all_to_all(packed, 'head', split_axis=1, concat_axis=0, tiled=True)]
  transfers between devices with their start and end apart: 4 -> 0, of which waited for: 3 -> 0; matrix products, arithmetic and copies ran while one was open for 34% -> 0% of each run, Pallas kernels for 0% -> 0%
where the time goes in v1:
time: 101 us
  Pallas kernels  87.4 us (87%)
  local copies, waits for them, and re-layouts  11.7 us (12%)
  between operations  1.32 us (1%)
    pallas_call x1, Pallas kernels, step(): pl.pallas_call(kernel, out_shape=(jax.ShapeDtypeStruct((own, width), BF16...  87.4 us
    unnamed x7, local copies, waits for them, and re-layouts  6.9 us

profile of v1, /device:TPU:1, one launch (start us, length us, event | category | flops | bytes accessed | tf_op | source)
XLA Modules:
  0.0 101.1 jit_solution(11764973225232836300)
XLA Ops:
  0.6 0.0 copy-start
  0.6 1.3 %dynamic_slice.8 = s32[1]{0:T(128)} dynamic-slice(s32[16]{0:T(128)} %prefix_len.1, s32[]{:T(128)S(6)} %select_n.8), dynamic_slice_sizes={1} | dynamic-slice | bytes 12 | tf_op jit(solution)/shard_map/jit(dynamic_index_in_dim)/dynamic_slice | solution.py:434
  2.6 0.7 multiply_sine_fusion
  3.3 1.3 %reshape.23.gain = f32[1,2560]{1,0:T(1,128)} reshape(f32[2560]{0:T(1024)} %param.11) | data formatting | bytes 20480 | tf_op jit(solution)/shard_map/reshape | solution.py:469
  4.7 0.7 broadcast_in_dim.5.sin_pre
  5.3 0.7 broadcast_in_dim.4.cos_pre
  6.0 0.0 copy-done
  6.0 0.8 constant_dynamic-slice_fusion.w_mine
  6.8 3.7 %copy.12 = bf16[1,4096,160]{2,1,0:T(8,128)(2,1)} copy(bf16[1,4096,160]{1,2,0:T(8,128)(2,1)} %param.14) | data formatting | bytes 2621440 | tf_op args[4]
  10.5 87.4 %shard_map.113 = (bf16[192,2560]{1,0:T(8,128)(2,1)}, bf16[1536,160]{1,0:T(8,128)(2,1)}) custom-call(bf16[192,2560]{1,0:T(8,128)(2,1)} %bitcast.7, f32[1,2560]{1,0:T(1,128)} %reshape.23.gain, bf16[160,480]{1,0:T(8,128)(2,1)} %constant_dynamic-slice_fusion.w_mine, bf16[160,2560]{1,0:T(8,128)(2,1)} %bitcast.9, bf16[4096,160]{1,0:T(8,128)(2,1)} %bitcast.6, ...), custom_call_target="tpu_custom_call" | custom-call | tf_op jit(solution)/shard_map/pallas_call | solution.py:442
  97.9 0.0 copy-start.1
  97.9 2.2 %copy.13 = bf16[1,1536,160]{1,2,0:T(8,128)(2,1)} copy(bf16[1,1536,160]{2,1,0:T(8,128)(2,1)} %bitcast.10) | data formatting | bytes 983040
  100.1 0.0 copy-done.1
  100.1 0.9 copy.15
Async XLA Ops:
  0.6 5.4 %copy-start = (bf16[160,3840]{1,0:T(8,128)(2,1)S(1)}, bf16[160,3840]{1,0:T(8,128)(2,1)}, u32[]{:S(2)}) copy-start(bf16[160,3840]{1,0:T(8,128)(2,1)} %param.12) | copy-start | bytes 3686404
  97.9 2.3 %copy-start.1 = (bf16[192,2560]{1,0:T(8,128)(2,1)S(1)}, bf16[192,2560]{1,0:T(8,128)(2,1)}, u32[]{:S(2)}) copy-start(bf16[192,2560]{1,0:T(8,128)(2,1)} %get-tuple-element.4) | copy-start | bytes 2949124

commit v2 on v1

--- a/solution.py
+++ b/solution.py
@@ -13,6 +13,7 @@
 GROUP = 4
 WINDOW = 4096
 QBLOCK = 128
+SPLITS = ((80, 80),)
 HIDE = -(2.0**127)
 F32 = jnp.float32
 BF16 = jnp.bfloat16
@@ -24,10 +25,11 @@
 
 
 def kernel(
-    hidden, gain, w_mine, wo_mine, kv, cos_slot, sin_slot, cos_pre, sin_pre, new_len, prefix_len,
+    hidden_hbm, gain, w_mine, wo_mine, kv_hbm, cos_hbm, sin_hbm, frequency, new_len, prefix_len,
     out, written,
-    rows, wq, wo, keys, vals, queries, state, maxes, ready, landed, finished,
-    w_send, w_recv, o_send, o_recv, p_send, p_recv, y_send, y_recv, a_send, a_recv,
+    hidden, cos_slot, sin_slot, cached_keys,
+    rows, wq, wo, keys, vals, queries, state, maxes, ready, received, landed, turned,
+    local, w_send, w_recv, o_send, o_recv, p_send, p_recv, y_send, y_recv, a_send, a_recv,
 ):
     s = lax.axis_index("seq")
     h = lax.axis_index("head")
@@ -42,6 +44,22 @@
     a, b = x + c * (z - x), z + c * (x - z)
     step_a, step_b = 4 - 3 * c, 1 + 3 * c
 
+    fetches = []
+
+    def fetch(src, dst):
+        copy = pltpu.make_async_copy(src, dst, local.at[len(fetches)])
+        copy.start()
+        fetches.append(copy)
+        return copy
+
+    got_hidden = fetch(hidden_hbm, hidden)
+    got_wq = fetch(w_mine, wq.at[pl.ds(pl.multiple_of(s * piece, 16), piece)])
+    got_keys = fetch(kv_hbm.at[pl.ds(0, HEAD_DIM)], cached_keys)
+    got_vals = fetch(kv_hbm.at[pl.ds(HEAD_DIM, HEAD_DIM)], vals.at[pl.ds(0, HEAD_DIM), pl.ds(0, WINDOW)])
+    got_wo = fetch(wo_mine, wo.at[pl.ds(pl.multiple_of(s * piece, 16), piece)])
+    got_cos = fetch(cos_hbm, cos_slot)
+    got_sin = fetch(sin_hbm, sin_slot)
+
     def slot(da, db):
         return lax.rem(a + da + 4, 4) * step_a + lax.rem(b + db + 4, 4) * step_b
 
@@ -64,17 +82,20 @@
     turns = (0, -1, 1, 2)
 
     class Gather:
-        def __init__(self, mine, whole, first, second, send, recv):
+        def __init__(self, mine, whole, first, second, send, recv, at=0):
             self.mine, self.whole, self.first, self.second = mine, whole, first, second
-            self.send, self.recv = send, recv
+            self.send, self.recv, self.at = send, recv, at
 
         def copy(self, m, src, dst, da, db):
-            return remote(src, dst, self.send.at[m], self.recv.at[m], slot(da, db), h)
-
-        def start_own(self):
+            return remote(src, dst, self.send.at[self.at + m], self.recv.at[self.at + m], slot(da, db), h)
+
+        def start_a(self):
             me = self.whole(slot(0, 0))
             self.copy(0, self.mine, me, 1, 0).start()
             self.copy(1, self.mine, me, -1, 0).start()
+
+        def start_b(self):
+            me = self.whole(slot(0, 0))
             self.copy(4, self.mine, me, 0, 1).start()
             self.copy(5, self.mine, me, 0, -1).start()
 
@@ -100,8 +121,8 @@
             self.got(3, self.second(slot(2, 0)))
             self.forward_b(3)
 
-        def fourth_step(self):
-            for q in range(4):
+        def fourth_step(self, shards):
+            for q in shards:
                 self.got(4 + 2 * q, self.whole(slot(turns[q], -1)))
                 self.got(5 + 2 * q, self.whole(slot(turns[q], 1)))
                 ra, rb = self.first(slot(turns[q], -1)), self.second(slot(turns[q], 1))
@@ -130,7 +151,15 @@
     def wq_rows(offset, count):
         return lambda sl: wq.at[pl.ds(pl.multiple_of(sl * piece + offset, 16), count)]
 
-    gather_q = Gather(w_mine, wq_rows(0, piece), wq_rows(0, piece // 2), wq_rows(piece // 2, piece // 2), w_send, w_recv)
+    gathers_q, at = [], 0
+    for i, (one, two) in enumerate(SPLITS):
+        gathers_q.append(
+            Gather(
+                wq_rows(at, one + two)(s), wq_rows(at, one + two), wq_rows(at, one), wq_rows(at + one, two),
+                w_send, w_recv, 20 * i,
+            )
+        )
+        at += one + two
 
     def wo_part(core, lo, count):
         return lambda sl: wo.at[
@@ -146,7 +175,11 @@
         region = wo_part(core, 0, width)(sl)
         return remote(region, region, p_send.at[sl], p_recv.at[sl], s, head_of(0, 1 - c))
 
-    gather_q.start_own()
+    got_wq.wait()
+    for gather_q in gathers_q:
+        gather_q.start_a()
+        gather_q.start_b()
+    got_hidden.wait()
 
     def row_block(dy, core, offset=0, count=own):
         return rows.at[lax.rem(y + dy + 4, 4), pl.ds(pl.multiple_of(core * own + offset, 16), count)]
@@ -154,7 +187,7 @@
     def norm_rows(i, carry):
         values = hidden[pl.ds(pl.multiple_of(i * 32, 32), 32), :].astype(F32)
         meansq = jnp.mean(values * values, axis=-1, keepdims=True)
-        normed = (values * lax.rsqrt(meansq + 1e-05) * gain[...]).astype(BF16)
+        normed = (values * lax.rsqrt(meansq + 1e-05) * gain[...].reshape(1, width)).astype(BF16)
         rows[y, pl.ds(pl.multiple_of(c * own + i * 32, 32), 32), :] = normed
         return carry
 
@@ -163,27 +196,35 @@
     def y_copy(m, region, dy, core):
         return remote(region, region, y_send.at[m], y_recv.at[m], s, head_of(dy, core))
 
-    y_copy(1, row_block(0, c), 1, c).start()
-    y_copy(2, row_block(0, c), -1, c).start()
+    half = own // 2
+    y_copy(1, row_block(0, c, 0, half), 1, c).start()
+    y_copy(3, row_block(0, c, half, half), -1, c).start()
+    y_copy(2, row_block(0, c, half, half), 1, c).start()
+    y_copy(4, row_block(0, c, 0, half), -1, c).start()
     y_copy(0, row_block(0, c), 0, 1 - c).start()
 
-    wq[pl.ds(pl.multiple_of(s * piece, 16), piece), :] = w_mine[...]
-    wo[pl.ds(pl.multiple_of(s * piece, 16), piece), :] = wo_mine[...]
+    for gather_q in gathers_q:
+        gather_q.second_step()
+    got_keys.wait()
 
     def prepare_cache(i, carry):
         at = pl.ds(pl.multiple_of(i * 256, 256), 256)
-        block = kv[at, :].astype(F32)
-        low = block[:, :128]
+        token = i * 256 + lax.broadcasted_iota(jnp.int32, (48, 256), 1)
+        first = lax.broadcasted_iota(jnp.int32, (48, 256), 0) == 0
+        bias = jnp.where(first & (token < WINDOW - prefix), HIDE, 0.0)
+        block = jnp.transpose(jnp.concatenate([cached_keys[:, at].astype(F32), bias], axis=0))
         lane = lax.broadcasted_iota(jnp.int32, (256, 128), 1)
-        position = i * 256 + lax.broadcasted_iota(jnp.int32, (256, 128), 0)
-        hidden_slot = (lane == HEAD_DIM) & (position < WINDOW - prefix)
-        key = jnp.where(lane < HEAD_DIM, low, 0.0)
-        keys[at, :128] = jnp.where(hidden_slot, HIDE, key).astype(BF16)
-        keys[at, 128:] = key.astype(BF16)
-        vals[:HEAD_DIM, at] = jnp.transpose(block)[HEAD_DIM:, :].astype(BF16)
+        keys[at, :128] = block.astype(BF16)
+        keys[at, 128:] = jnp.where(lane < HEAD_DIM, block, 0.0).astype(BF16)
         return carry
 
     lax.fori_loop(0, WINDOW // 256, prepare_cache, 0)
+    for gather_q in gathers_q:
+        gather_q.third_step()
+    got_wo.wait()
+    got_vals.wait()
+    got_cos.wait()
+    got_sin.wait()
     total = vals.shape[1]
     one_row = (lax.broadcasted_iota(jnp.int32, (16, 512), 0) == 0).astype(F32).astype(BF16)
     for i in range(total // 512):
@@ -194,13 +235,22 @@
             queries[k, 80:96, cols] = one_row
             queries[k, 96:128, cols] = jnp.zeros((32, 512), BF16)
             queries[k, 208:256, cols] = jnp.zeros((48, 512), BF16)
-
-    gather_q.second_step()
-    gather_q.third_step()
-    gather_q.fourth_step()
-    gather_o.start_own()
+    turn_pre = frequency[...] * prefix.astype(F32)
+    cp, sp = jnp.cos(turn_pre)[:, 0:1], jnp.sin(turn_pre)[:, 0:1]
+
+    for gather_q in gathers_q:
+        gather_q.fourth_step(range(4))
+    gather_o.start_a()
+    gather_o.start_b()
     y_copy(0, row_block(0, 1 - c), 0, c).wait_recv()
-    gather_q.last_step()
+    y_copy(1, row_block(-1, c, 0, half), 0, c).wait_recv()
+    y_copy(5, row_block(-1, c, 0, half), 1, c).start()
+    y_copy(3, row_block(1, c, half, half), 0, c).wait_recv()
+    y_copy(6, row_block(1, c, half, half), -1, c).start()
+    y_copy(7, row_block(-1, c, 0, half), 0, 1 - c).start()
+    y_copy(9, row_block(1, c, half, half), 0, 1 - c).start()
+    for gather_q in gathers_q:
+        gather_q.last_step()
 
     scale = math.log2(math.e) / math.sqrt(HEAD_DIM)
 
@@ -208,7 +258,6 @@
         projected = jnp.transpose(matmul(rows[yk], wq[...]))
         tokens = pl.ds(pl.multiple_of(yk * chip, 128), chip)
         cn, sn = cos_slot[:, tokens], sin_slot[:, tokens]
-        cp, sp = cos_pre[:, 0:1], sin_pre[:, 0:1]
         cosine, sine = cn * cp - sn * sp, sn * cp + cn * sp
 
         def rotate(at):
@@ -229,11 +278,10 @@
         value = projected[(GROUP + 1) * HEAD_DIM : (GROUP + 2) * HEAD_DIM].astype(BF16)
         slots = pl.ds(pl.multiple_of(WINDOW + yk * chip, 128), chip)
         vals[:HEAD_DIM, slots] = value
-        pair = jnp.transpose(jnp.concatenate([key, value.astype(F32)], axis=0))
-        index = yk * chip + lax.broadcasted_iota(jnp.int32, pair.shape, 0)
-        written[tokens, :] = jnp.where(index < length, pair, 0.0).astype(BF16)
-        lane = lax.broadcasted_iota(jnp.int32, (chip, 128), 1)
-        clean = jnp.where(lane < HEAD_DIM, pair[:, :128], 0.0).astype(BF16)
+        pair = jnp.concatenate([key, value.astype(F32)], axis=0)
+        index = yk * chip + lax.broadcasted_iota(jnp.int32, pair.shape, 1)
+        written[:, tokens] = jnp.where(index < length, pair, 0.0).astype(BF16)
+        clean = jnp.transpose(jnp.concatenate([key, jnp.zeros((48, chip), F32)], axis=0)).astype(BF16)
         keys[slots, :128] = clean
         keys[slots, 128:] = clean
 
@@ -313,42 +361,46 @@
                 sums = carry[1]
                 attended = sums[:HEAD_DIM] * (1.0 / sums[HEAD_DIM : HEAD_DIM + 1])
                 token = base + j * 128 + (lax.broadcasted_iota(jnp.int32, (HEAD_DIM, 512), 1) & (QBLOCK - 1))
-                attended = jnp.where(token < length, attended, 0.0).astype(BF16)
-                for g in range(GROUP):
-                    ready[yk, g * HEAD_DIM : (g + 1) * HEAD_DIM, j * 128 : (j + 1) * 128] = attended[:, g * 128 : (g + 1) * 128]
+                attended = jnp.where(token < length, attended, 0.0)
+                heads = [attended[:, g * 128 : (g + 1) * 128] for g in range(GROUP)]
+                if j == 1:
+                    left = lax.broadcasted_iota(jnp.int32, (HEAD_DIM, 128), 1) < 64
+                    for p in range(2):
+                        one, two = heads[p], heads[p + 2]
+                        at = slice(320 + p * HEAD_DIM, 320 + (p + 1) * HEAD_DIM)
+                        ready[yk, 0, at, :] = jnp.where(left, one, pltpu.roll(two, 64, 1)).astype(BF16)
+                        ready[yk, 1, at, :] = jnp.where(left, pltpu.roll(one, 64, 1), two).astype(BF16)
+                else:
+                    for g in range(GROUP):
+                        ready[yk, j // 2, g * HEAD_DIM : (g + 1) * HEAD_DIM, :] = heads[g].astype(BF16)
             sc = later
 
     def arrive(k):
         @pl.when(k == 1)
         def _():
-            y_copy(1, row_block(-1, c), 0, c).wait_recv()
-            y_copy(2, row_block(1, c), 0, c).wait_recv()
-            r = row_block(-1, c, 0, own // 2)
-            y_copy(5, r, 1, c).start()
-            r = row_block(1, c, own // 2, own // 2)
-            y_copy(6, r, -1, c).start()
-            y_copy(3, row_block(-1, c), 0, 1 - c).start()
-            y_copy(4, row_block(1, c), 0, 1 - c).start()
+            y_copy(2, row_block(-1, c, half, half), 0, c).wait_recv()
+            y_copy(8, row_block(-1, c, half, half), 0, 1 - c).start()
+            y_copy(4, row_block(1, c, 0, half), 0, c).wait_recv()
+            y_copy(10, row_block(1, c, 0, half), 0, 1 - c).start()
             gather_o.second_step()
-            y_copy(3, row_block(-1, 1 - c), 0, c).wait_recv()
+            y_copy(7, row_block(-1, 1 - c, 0, half), 0, c).wait_recv()
+            y_copy(8, row_block(-1, 1 - c, half, half), 0, c).wait_recv()
 
         @pl.when(k == 2)
         def _():
             gather_o.third_step()
-            y_copy(4, row_block(1, 1 - c), 0, c).wait_recv()
+            y_copy(9, row_block(1, 1 - c, half, half), 0, c).wait_recv()
+            y_copy(10, row_block(1, 1 - c, 0, half), 0, c).wait_recv()
 
         @pl.when(k == 3)
         def _():
-            y_copy(5, row_block(2, c, 0, own // 2), 0, c).wait_recv()
-            y_copy(6, row_block(2, c, own // 2, own // 2), 0, c).wait_recv()
-            y_copy(7, row_block(2, c), 0, 1 - c).start()
-            gather_o.fourth_step()
+            y_copy(5, row_block(2, c, 0, half), 0, c).wait_recv()
+            y_copy(6, row_block(2, c, half, half), 0, c).wait_recv()
+            y_copy(11, row_block(2, c), 0, 1 - c).start()
+            gather_o.fourth_step((0, 1, 2))
             for q in range(1, 4):
                 partner_copy(slot(turns[q], 0), c).start()
-            for q in range(4):
-                partner_copy(slot(turns[q], -1), c).start()
-                partner_copy(slot(turns[q], 1), c).start()
-            y_copy(7, row_block(2, 1 - c), 0, c).wait_recv()
+            y_copy(11, row_block(2, 1 - c), 0, c).wait_recv()
 
     def first_loop(k, carry):
         arrive(k)
@@ -361,15 +413,25 @@
     lax.fori_loop(0, 4, first_loop, 0)
 
     def attended_copy(yk, core):
-        src = ready.at[yk, :, pl.ds(pl.multiple_of(core * 128, 128), 256)]
-        dst = landed.at[pl.ds(pl.multiple_of(h * GROUP * HEAD_DIM, 16), GROUP * HEAD_DIM)]
-        return remote(src, dst, a_send.at[2 * yk + core], a_recv.at[h], s, 2 * yk + core)
+        return remote(
+            ready.at[yk, core], received.at[h], a_send.at[2 * yk + core], a_recv.at[h], s, 2 * yk + core
+        )
 
     def second_loop(k, carry):
         turn = jnp.where(k == 0, 2, jnp.where(k == 1, 1, jnp.where(k == 2, 3, 0)))
         yk = lax.rem(y + turn, 4)
 
+        @pl.when(k == 0)
+        def _():
+            gather_o.fourth_step((3,))
+
         @pl.when(k == 1)
+        def _():
+            for q in range(4):
+                partner_copy(slot(turns[q], -1), c).start()
+                partner_copy(slot(turns[q], 1), c).start()
+
+        @pl.when(k == 2)
         def _():
             gather_o.last_step()
             for q in range(4):
@@ -389,33 +451,42 @@
         return carry
 
     lax.fori_loop(0, 4, second_loop, 0)
-    mine = pl.ds(pl.multiple_of(h * GROUP * HEAD_DIM, 16), GROUP * HEAD_DIM)
-    landed[mine, :] = ready[y, :, pl.ds(pl.multiple_of(c * 128, 128), 256)]
+
+    def unpack(src_head, block):
+        top = src_head * GROUP * HEAD_DIM
+        landed[pl.ds(pl.multiple_of(top, 16), GROUP * HEAD_DIM), :128] = block[: GROUP * HEAD_DIM]
+        packed = block[GROUP * HEAD_DIM :]
+        landed[pl.ds(pl.multiple_of(top, 16), 2 * HEAD_DIM), 128:] = packed
+        turned_back = pltpu.roll(packed.astype(F32), 64, 1).astype(BF16)
+        landed[pl.ds(pl.multiple_of(top + 2 * HEAD_DIM, 16), 2 * HEAD_DIM), 128:] = turned_back
+
+    unpack(h, ready[y, c])
     for d in range(1, 16):
         sl = lax.rem(s + d, 16)
         partner_copy(sl, 1 - c).wait_recv()
-    for d in range(1, 8):
-        src = lax.rem(h + d, 8)
-        region = landed.at[pl.ds(pl.multiple_of(src * GROUP * HEAD_DIM, 16), GROUP * HEAD_DIM)]
-        remote(region, region, a_send.at[0], a_recv.at[src], s, h).wait_recv()
-
+
+    for dy, core in ((0, 1 - c), (2, 0), (2, 1), (1, 0), (1, 1), (-1, 0), (-1, 1)):
+        src = head_of(dy, core)
+        remote(received.at[src], received.at[src], a_send.at[0], a_recv.at[src], s, h).wait_recv()
+        unpack(src, received[src])
     for i in range(width // 512):
-        block = matmul(wo[i * 512 : (i + 1) * 512, :], landed[...])
-        finished[:, i * 512 : (i + 1) * 512] = jnp.transpose(block)
-    out[...] = finished[pl.ds(pl.multiple_of(c * (256 - own), 64), own), :].astype(BF16)
-
-    gather_q.drain()
+        turned[:, i * 512 : (i + 1) * 512] = jnp.transpose(matmul(wo[i * 512 : (i + 1) * 512, :], landed[...]))
+    rest = own - 128
+    out[pl.ds(pl.multiple_of(c * rest, 64), 128), :] = turned[:128, :].astype(BF16)
+    out[pl.ds(pl.multiple_of((1 - c) * 128, 64), rest), :] = turned[128:own, :].astype(BF16)
+
+    for gather_q in gathers_q:
+        gather_q.drain()
     gather_o.drain()
     for d in range(1, 16):
         partner_copy(lax.rem(s + d, 16), c).wait_send()
-    for m in (0, 1, 2, 3, 4, 7):
+    for m in (0, 11):
         y_copy(m, row_block(0, c), 0, 1 - c).wait_send()
-    for m in (5, 6):
-        y_copy(m, row_block(0, c, 0, own // 2), 0, 1 - c).wait_send()
+    for m in range(1, 11):
+        y_copy(m, row_block(0, c, 0, half), 0, 1 - c).wait_send()
     for d in range(1, 8):
         dst = lax.rem(h + d, 8)
-        region = landed.at[pl.ds(0, GROUP * HEAD_DIM)]
-        remote(region, region, a_send.at[dst], a_recv.at[0], s, dst).wait_send()
+        remote(received.at[0], received.at[0], a_send.at[dst], a_recv.at[0], s, dst).wait_send()
 
 
 def solution(mesh):
@@ -427,27 +498,30 @@
         piece = w_qkv.shape[0]
         w_mine = lax.dynamic_slice(w_qkv, (0, h * wide), (piece, wide))
         wo_mine = w_out.T
+        cached = jnp.swapaxes(kv_cache.reshape(WINDOW, 2 * HEAD_DIM), 0, 1)
         frequency = np.exp(np.arange(HALF, dtype=np.float64) * (-2.0 * math.log(10000.0) / HEAD_DIM))
         angles = frequency[:, None] * np.arange(new_total, dtype=np.float64)[None, :]
         cos_slot = jnp.asarray(np.cos(angles).astype(np.float32))
         sin_slot = jnp.asarray(np.sin(angles).astype(np.float32))
-        prefix = lax.dynamic_index_in_dim(prefix_len, s, 0, keepdims=False).astype(F32)
-        turn = prefix * jnp.asarray(frequency.astype(np.float32))
-        cos_pre = jnp.broadcast_to(jnp.cos(turn)[:, None], (HALF, 128))
-        sin_pre = jnp.broadcast_to(jnp.sin(turn)[:, None], (HALF, 128))
+        lanes = jnp.asarray(np.broadcast_to(frequency[:, None], (HALF, 128)).astype(np.float32))
         chip = 2 * own
         dma = pltpu.SemaphoreType.DMA
         vmem = pl.BlockSpec(memory_space=pltpu.VMEM)
         smem = pl.BlockSpec(memory_space=pltpu.SMEM)
+        any_ = pl.BlockSpec(memory_space=pl.ANY)
         attn_out, kv_written = pl.pallas_call(
             kernel,
             out_shape=(
-                jax.ShapeDtypeStruct((own, width), BF16),
-                jax.ShapeDtypeStruct((new_total, 2 * HEAD_DIM), BF16),
+                pltpu.VMEM((own, width), BF16),
+                pltpu.VMEM((2 * HEAD_DIM, new_total), BF16),
             ),
-            in_specs=[vmem] * 9 + [smem] * 2,
+            in_specs=[any_, vmem, any_, any_, any_, any_, any_, vmem, smem, smem],
             out_specs=(vmem, vmem),
             scratch_shapes=[
+                pltpu.VMEM((own, width), BF16),
+                pltpu.VMEM((HALF, new_total), F32),
+                pltpu.VMEM((HALF, new_total), F32),
+                pltpu.VMEM((HEAD_DIM, WINDOW), BF16),
                 pltpu.VMEM((4, chip, width), BF16),
                 pltpu.VMEM((16 * piece, wide), BF16),
                 pltpu.VMEM((16 * piece, width), BF16),
@@ -456,20 +530,21 @@
                 pltpu.VMEM((4, 256, 4 * chip), BF16),
                 pltpu.VMEM((4, 88, 4 * chip), F32),
                 pltpu.VMEM((4, 1, 4 * chip), F32),
-                pltpu.VMEM((4, GROUP * HEAD_DIM, chip), BF16),
+                pltpu.VMEM((4, 2, 6 * HEAD_DIM, 128), BF16),
+                pltpu.VMEM((8, 6 * HEAD_DIM, 128), BF16),
                 pltpu.VMEM((8 * GROUP * HEAD_DIM, 256), BF16),
                 pltpu.VMEM((256, width), F32),
-                dma((20,)), dma((20,)), dma((20,)), dma((20,)), dma((16,)), dma((16,)),
-                dma((8,)), dma((8,)), dma((8,)), dma((8,)),
+                dma((7,)), dma((20 * len(SPLITS),)), dma((20 * len(SPLITS),)), dma((20,)), dma((20,)), dma((16,)), dma((16,)),
+                dma((12,)), dma((12,)), dma((8,)), dma((8,)),
             ],
             compiler_params=pltpu.CompilerParams(
-                collective_id=0, has_side_effects=True, vmem_limit_bytes=62 * 1024 * 1024
+                collective_id=0, has_side_effects=True, vmem_limit_bytes=56 * 1024 * 1024
             ),
         )(
-            hidden.reshape(own, width), norm_gain.reshape(1, width), w_mine, wo_mine,
-            kv_cache.reshape(WINDOW, 2 * HEAD_DIM), cos_slot, sin_slot, cos_pre, sin_pre, new_len, prefix_len,
+            hidden.reshape(own, width), norm_gain, w_mine, wo_mine,
+            cached, cos_slot, sin_slot, lanes, new_len, prefix_len,
         )
-        return attn_out.reshape(1, own, width), kv_written.reshape(1, new_total, 2 * HEAD_DIM)
+        return attn_out.reshape(1, own, width), jnp.swapaxes(kv_written, 0, 1).reshape(1, new_total, 2 * HEAD_DIM)
 
     return jax.shard_map(
         step,

time: 101 us -> 86.7 us (0.86)
  local copies, waits for them, and re-layouts: 11.7 us -> 3.79 us
  Pallas kernels: 87.4 us -> 82 us
    pallas_call x1, Pallas kernels: 87.4 us -> 82 us  [step(): pl.pallas_call(kernel, out_shape=(pltpu.VMEM((own, width), BF16), pltpu.V...]
    unnamed x7 -> x4, local copies, waits for them, and re-layouts: 6.9 us -> 3.01 us
    broadcast_in_dim x2 -> x0, local copies, waits for them, and re-layouts: 1.35 us -> none  [the longest x1 0.68 us: step(): cos_pre = jnp.broadcast_to(jnp.cos(turn)[:, None], (HALF, 128))]
    dynamic_slice x1 -> x0, local copies, waits for them, and re-layouts: 1.34 us -> none  [step(): lax.dynamic_index_in_dim(prefix_len, s, 0, keepdims=False).astype(F32)]
    reshape x1 -> x0, local copies, waits for them, and re-layouts: 1.31 us -> none  [step(): norm_gain.reshape(1, width)]
where the time goes in v2:
time: 86.7 us; the launch traced here: 86.5 us
  Pallas kernels  82 us (95%)
  local copies, waits for them, and re-layouts  3.79 us (4%)
    pallas_call x1, Pallas kernels, step(): pl.pallas_call(kernel, out_shape=(pltpu.VMEM((own, width), BF16), pltpu.V...  82 us
    unnamed x4, local copies, waits for them, and re-layouts  3.01 us

profile of v2, /device:TPU:1, one launch (start us, length us, event | category | flops | bytes accessed | tf_op | source)
XLA Modules:
  0.0 86.5 jit_solution(2706627285495859794)
XLA Ops:
  0.6 0.0 copy-start
  0.6 1.3 %copy-done = bf16[160,3840]{1,0:T(8,128)(2,1)S(1)} copy-done((bf16[160,3840]{1,0:T(8,128)(2,1)S(1)}, bf16[160,3840]{1,0:T(8,128)(2,1)}, u32[]{:S(2)}) %copy-start) | copy-done | bytes 1228824
  1.9 0.8 constant_dynamic-slice_fusion.w_mine
  2.7 82.0 %shard_map.113 = (bf16[192,2560]{1,0:T(8,128)(2,1)S(1)}, bf16[160,1536]{1,0:T(8,128)(2,1)S(1)}) custom-call(bf16[192,2560]{1,0:T(8,128)(2,1)} %bitcast.12, f32[2560]{0:T(1024)} %gain.1, bf16[160,480]{1,0:T(8,128)(2,1)} %constant_dynamic-slice_fusion.w_mine, bf16[160,2560]{1,0:T(8,128)(2,1)} %bitcast.13, bf16[160,4096]{1,0:T(8,128)(2,1)} %bitcast.11, ...), custom_call_target="tpu_custom_call" | custom-call | tf_op jit(solution)/shard_map/pallas_call | solution.py:512
  84.7 0.9 %copy.14 = bf16[1,192,2560]{2,1,0:T(8,128)(2,1)} copy(bf16[1,192,2560]{2,1,0:T(8,128)(2,1)S(1)} %bitcast.9) | data formatting | bytes 1966080
  85.7 0.8 copy.15
Async XLA Ops:
  0.6 1.3 %copy-start = (bf16[160,3840]{1,0:T(8,128)(2,1)S(1)}, bf16[160,3840]{1,0:T(8,128)(2,1)}, u32[]{:S(2)}) copy-start(bf16[160,3840]{1,0:T(8,128)(2,1)} %param.12) | copy-start | bytes 3686404

commit v3 on v2

--- a/solution.py
+++ b/solution.py
@@ -73,18 +73,18 @@
         )
 
     barrier = pltpu.get_barrier_semaphore()
-    for da, db in ((1, 0), (-1, 0), (0, 1), (0, -1)):
+    for da, db in ((1, 0), (-1, 0), (2, 0), (0, 1), (0, -1)):
         pl.semaphore_signal(barrier, inc=1, device_id={"seq": slot(da, db), "head": h}, device_id_type=MESH)
     for d in range(1, 8):
         pl.semaphore_signal(barrier, inc=1, device_id={"seq": s, "head": lax.rem(h + d, 8)}, device_id_type=MESH)
-    pl.semaphore_wait(barrier, 11)
+    pl.semaphore_wait(barrier, 12)
 
     turns = (0, -1, 1, 2)
 
     class Gather:
-        def __init__(self, mine, whole, first, second, send, recv, at=0):
+        def __init__(self, mine, whole, first, second, send, recv, at=0, direct=False):
             self.mine, self.whole, self.first, self.second = mine, whole, first, second
-            self.send, self.recv, self.at = send, recv, at
+            self.send, self.recv, self.at, self.direct = send, recv, at, direct
 
         def copy(self, m, src, dst, da, db):
             return remote(src, dst, self.send.at[self.at + m], self.recv.at[self.at + m], slot(da, db), h)
@@ -93,6 +93,8 @@
             me = self.whole(slot(0, 0))
             self.copy(0, self.mine, me, 1, 0).start()
             self.copy(1, self.mine, me, -1, 0).start()
+            if self.direct:
+                self.copy(2, self.mine, me, 2, 0).start()
 
         def start_b(self):
             me = self.whole(slot(0, 0))
@@ -110,15 +112,19 @@
         def second_step(self):
             self.got(0, self.whole(slot(-1, 0)))
             self.got(1, self.whole(slot(1, 0)))
-            ra, rb = self.first(slot(-1, 0)), self.second(slot(1, 0))
-            self.copy(2, ra, ra, 1, 0).start()
-            self.copy(3, rb, rb, -1, 0).start()
+            if not self.direct:
+                ra, rb = self.first(slot(-1, 0)), self.second(slot(1, 0))
+                self.copy(2, ra, ra, 1, 0).start()
+                self.copy(3, rb, rb, -1, 0).start()
             self.forward_b(1)
             self.forward_b(2)
 
         def third_step(self):
-            self.got(2, self.first(slot(2, 0)))
-            self.got(3, self.second(slot(2, 0)))
+            if self.direct:
+                self.got(2, self.whole(slot(2, 0)))
+            else:
+                self.got(2, self.first(slot(2, 0)))
+                self.got(3, self.second(slot(2, 0)))
             self.forward_b(3)
 
         def fourth_step(self, shards):
@@ -136,12 +142,12 @@
 
         def drain(self):
             me = self.mine
-            for m in (0, 1, 4, 5):
+            for m in (0, 1, 2, 4, 5) if self.direct else (0, 1, 4, 5):
                 self.copy(m, me, me, 1, 0).wait_send()
-            for m in (2, 12, 14, 16, 18):
+            for m in (12, 14, 16, 18) if self.direct else (2, 12, 14, 16, 18):
                 r = self.first(slot(0, 0))
                 self.copy(m, r, r, 1, 0).wait_send()
-            for m in (3, 13, 15, 17, 19):
+            for m in (13, 15, 17, 19) if self.direct else (3, 13, 15, 17, 19):
                 r = self.second(slot(0, 0))
                 self.copy(m, r, r, 1, 0).wait_send()
             for m in (6, 7, 8, 9, 10, 11):
@@ -156,7 +162,7 @@
         gathers_q.append(
             Gather(
                 wq_rows(at, one + two)(s), wq_rows(at, one + two), wq_rows(at, one), wq_rows(at + one, two),
-                w_send, w_recv, 20 * i,
+                w_send, w_recv, 20 * i, direct=True,
             )
         )
         at += one + two
@@ -241,7 +247,6 @@
     for gather_q in gathers_q:
         gather_q.fourth_step(range(4))
     gather_o.start_a()
-    gather_o.start_b()
     y_copy(0, row_block(0, 1 - c), 0, c).wait_recv()
     y_copy(1, row_block(-1, c, 0, half), 0, c).wait_recv()
     y_copy(5, row_block(-1, c, 0, half), 1, c).start()
@@ -251,6 +256,7 @@
     y_copy(9, row_block(1, c, half, half), 0, 1 - c).start()
     for gather_q in gathers_q:
         gather_q.last_step()
+    gather_o.start_b()
 
     scale = math.log2(math.e) / math.sqrt(HEAD_DIM)
 
@@ -397,7 +403,7 @@
             y_copy(5, row_block(2, c, 0, half), 0, c).wait_recv()
             y_copy(6, row_block(2, c, half, half), 0, c).wait_recv()
             y_copy(11, row_block(2, c), 0, 1 - c).start()
-            gather_o.fourth_step((0, 1, 2))
+            gather_o.fourth_step((0,))
             for q in range(1, 4):
                 partner_copy(slot(turns[q], 0), c).start()
             y_copy(11, row_block(2, 1 - c), 0, c).wait_recv()
@@ -423,15 +429,16 @@
 
         @pl.when(k == 0)
         def _():
+            gather_o.fourth_step((1, 2))
+
+        @pl.when(k == 1)
+        def _():
             gather_o.fourth_step((3,))
-
-        @pl.when(k == 1)
-        def _():
             for q in range(4):
                 partner_copy(slot(turns[q], -1), c).start()
                 partner_copy(slot(turns[q], 1), c).start()
 
-        @pl.when(k == 2)
+        @pl.when(k == 3)
         def _():
             gather_o.last_step()
             for q in range(4):

time: 86.7 us -> 85.3 us (0.984)
  Pallas kernels: 82 us -> 80.7 us
    pallas_call x1, Pallas kernels: 82 us -> 80.7 us  [step(): pl.pallas_call(kernel, out_shape=(pltpu.VMEM((own, width), BF16), pltpu.V...]
where the time goes in v3:
time: 85.3 us; the launch traced here: 85.1 us
  Pallas kernels  80.7 us (95%)
  local copies, waits for them, and re-layouts  3.79 us (4%)
    pallas_call x1, Pallas kernels, step(): pl.pallas_call(kernel, out_shape=(pltpu.VMEM((own, width), BF16), pltpu.V...  80.7 us
    unnamed x4, local copies, waits for them, and re-layouts  3.01 us

profile of v3, /device:TPU:1, one launch (start us, length us, event | category | flops | bytes accessed | tf_op | source)
XLA Modules:
  0.0 85.1 jit_solution(8478030335172260020)
XLA Ops:
  0.6 0.0 copy-start
  0.6 1.3 %copy-done = bf16[160,3840]{1,0:T(8,128)(2,1)S(1)} copy-done((bf16[160,3840]{1,0:T(8,128)(2,1)S(1)}, bf16[160,3840]{1,0:T(8,128)(2,1)}, u32[]{:S(2)}) %copy-start) | copy-done | bytes 1228824
  1.9 0.8 constant_dynamic-slice_fusion.w_mine
  2.7 80.7 %shard_map.113 = (bf16[192,2560]{1,0:T(8,128)(2,1)S(1)}, bf16[160,1536]{1,0:T(8,128)(2,1)S(1)}) custom-call(bf16[192,2560]{1,0:T(8,128)(2,1)} %bitcast.12, f32[2560]{0:T(1024)} %gain.1, bf16[160,480]{1,0:T(8,128)(2,1)} %constant_dynamic-slice_fusion.w_mine, bf16[160,2560]{1,0:T(8,128)(2,1)} %bitcast.13, bf16[160,4096]{1,0:T(8,128)(2,1)} %bitcast.11, ...), custom_call_target="tpu_custom_call" | custom-call | tf_op jit(solution)/shard_map/pallas_call | solution.py:519
  83.4 0.9 %copy.14 = bf16[1,192,2560]{2,1,0:T(8,128)(2,1)} copy(bf16[1,192,2560]{2,1,0:T(8,128)(2,1)S(1)} %bitcast.9) | data formatting | bytes 1966080
  84.3 0.8 copy.15
Async XLA Ops:
  0.6 1.3 %copy-start = (bf16[160,3840]{1,0:T(8,128)(2,1)S(1)}, bf16[160,3840]{1,0:T(8,128)(2,1)}, u32[]{:S(2)}) copy-start(bf16[160,3840]{1,0:T(8,128)(2,1)} %param.12) | copy-start | bytes 3686404

commit v4 on v3

--- a/solution.py
+++ b/solution.py
@@ -13,6 +13,7 @@
 GROUP = 4
 WINDOW = 4096
 QBLOCK = 128
+COLS1, KEYS1 = 768, 512
 SPLITS = ((80, 80),)
 HIDE = -(2.0**127)
 F32 = jnp.float32
@@ -197,13 +198,14 @@
         rows[y, pl.ds(pl.multiple_of(c * own + i * 32, 32), 32), :] = normed
         return carry
 
-    lax.fori_loop(0, own // 32, norm_rows, 0)
 
     def y_copy(m, region, dy, core):
         return remote(region, region, y_send.at[m], y_recv.at[m], s, head_of(dy, core))
 
     half = own // 2
+    lax.fori_loop(0, half // 32, norm_rows, 0)
     y_copy(1, row_block(0, c, 0, half), 1, c).start()
+    lax.fori_loop(half // 32, own // 32, norm_rows, 0)
     y_copy(3, row_block(0, c, half, half), -1, c).start()
     y_copy(2, row_block(0, c, half, half), 1, c).start()
     y_copy(4, row_block(0, c, 0, half), -1, c).start()
@@ -310,26 +312,23 @@
         return top, total_
 
     common = 4 * chip
-    chunk1 = 512
 
     def first_phase(yk):
-        todo = [(j, common + i * chunk1) for j in range(3) for i in range((WINDOW - common) // chunk1)]
-        per = len(todo) // 3
+        keys_at = range(common, WINDOW, KEYS1)
+        todo = [(at, start) for at in range(0, 4 * chip, COLS1) for start in keys_at]
 
         def make(t):
-            j, start = todo[t]
-            return scores(start, chunk1, queries[yk, :, j * 512 : (j + 1) * 512])
+            at, start = todo[t]
+            return scores(start, KEYS1, queries[yk, :, at : at + COLS1])
 
         sc = make(0)
         carry = (None, None)
-        for t in range(len(todo)):
+        for t, (at, start) in enumerate(todo):
             later = make(t + 1) if t + 1 < len(todo) else None
-            j, start = todo[t]
-            carry = absorb(carry, sc, [(start, chunk1)])
-            if t % per == per - 1:
-                cols = slice(j * 512, (j + 1) * 512)
-                maxes[yk, :, cols] = carry[0]
-                state[yk, :, cols] = carry[1]
+            carry = absorb(carry, sc, [(start, KEYS1)])
+            if start + KEYS1 == WINDOW:
+                maxes[yk, :, at : at + COLS1] = carry[0]
+                state[yk, :, at : at + COLS1] = carry[1]
                 carry = (None, None)
             sc = later
 

time: 85.3 us -> 83 us (0.973)
  Pallas kernels: 80.7 us -> 78.4 us
    pallas_call x1, Pallas kernels: 80.7 us -> 78.4 us  [step(): pl.pallas_call(kernel, out_shape=(pltpu.VMEM((own, width), BF16), pltpu.V...]
where the time goes in v4:
time: 83 us; the launch traced here: 82.8 us
  Pallas kernels  78.4 us (94%)
  local copies, waits for them, and re-layouts  3.79 us (5%)
    pallas_call x1, Pallas kernels, step(): pl.pallas_call(kernel, out_shape=(pltpu.VMEM((own, width), BF16), pltpu.V...  78.4 us
    unnamed x4, local copies, waits for them, and re-layouts  3.01 us

profile of v4, /device:TPU:1, one launch (start us, length us, event | category | flops | bytes accessed | tf_op | source)
XLA Modules:
  0.0 82.8 jit_solution(14494167593226090118)
XLA Ops:
  0.6 0.0 copy-start
  0.6 1.3 %copy-done = bf16[160,3840]{1,0:T(8,128)(2,1)S(1)} copy-done((bf16[160,3840]{1,0:T(8,128)(2,1)S(1)}, bf16[160,3840]{1,0:T(8,128)(2,1)}, u32[]{:S(2)}) %copy-start) | copy-done | bytes 1228824
  1.9 0.8 constant_dynamic-slice_fusion.w_mine
  2.7 78.4 %shard_map.113 = (bf16[192,2560]{1,0:T(8,128)(2,1)S(1)}, bf16[160,1536]{1,0:T(8,128)(2,1)S(1)}) custom-call(bf16[192,2560]{1,0:T(8,128)(2,1)} %bitcast.12, f32[2560]{0:T(1024)} %gain.1, bf16[160,480]{1,0:T(8,128)(2,1)} %constant_dynamic-slice_fusion.w_mine, bf16[160,2560]{1,0:T(8,128)(2,1)} %bitcast.13, bf16[160,4096]{1,0:T(8,128)(2,1)} %bitcast.11, ...), custom_call_target="tpu_custom_call" | custom-call | tf_op jit(solution)/shard_map/pallas_call | solution.py:518
  81.1 0.9 %copy.14 = bf16[1,192,2560]{2,1,0:T(8,128)(2,1)} copy(bf16[1,192,2560]{2,1,0:T(8,128)(2,1)S(1)} %bitcast.9) | data formatting | bytes 1966080
  82.0 0.8 copy.15
Async XLA Ops:
  0.6 1.3 %copy-start = (bf16[160,3840]{1,0:T(8,128)(2,1)S(1)}, bf16[160,3840]{1,0:T(8,128)(2,1)}, u32[]{:S(2)}) copy-start(bf16[160,3840]{1,0:T(8,128)(2,1)} %param.12) | copy-start | bytes 3686404

commit v5 on v4

--- a/solution.py
+++ b/solution.py
@@ -467,14 +467,14 @@
         landed[pl.ds(pl.multiple_of(top + 2 * HEAD_DIM, 16), 2 * HEAD_DIM), 128:] = turned_back
 
     unpack(h, ready[y, c])
-    for d in range(1, 16):
-        sl = lax.rem(s + d, 16)
-        partner_copy(sl, 1 - c).wait_recv()
 
     for dy, core in ((0, 1 - c), (2, 0), (2, 1), (1, 0), (1, 1), (-1, 0), (-1, 1)):
         src = head_of(dy, core)
         remote(received.at[src], received.at[src], a_send.at[0], a_recv.at[src], s, h).wait_recv()
         unpack(src, received[src])
+    for d in range(1, 16):
+        sl = lax.rem(s + d, 16)
+        partner_copy(sl, 1 - c).wait_recv()
     for i in range(width // 512):
         turned[:, i * 512 : (i + 1) * 512] = jnp.transpose(matmul(wo[i * 512 : (i + 1) * 512, :], landed[...]))
     rest = own - 128

time: 83 us -> 83.2 us (level)
  no operation moved by 1% of the time
where the time goes in v5:
time: 83.2 us; the launch traced here: 83 us
  Pallas kernels  78.6 us (94%)
  local copies, waits for them, and re-layouts  3.79 us (5%)
    pallas_call x1, Pallas kernels, step(): pl.pallas_call(kernel, out_shape=(pltpu.VMEM((own, width), BF16), pltpu.V...  78.6 us
    unnamed x4, local copies, waits for them, and re-layouts  3.01 us

profile of v5, /device:TPU:1, one launch (start us, length us, event | category | flops | bytes accessed | tf_op | source)
XLA Modules:
  0.0 83.0 jit_solution(12631152282865267523)
XLA Ops:
  0.6 0.0 copy-start
  0.6 1.3 %copy-done = bf16[160,3840]{1,0:T(8,128)(2,1)S(1)} copy-done((bf16[160,3840]{1,0:T(8,128)(2,1)S(1)}, bf16[160,3840]{1,0:T(8,128)(2,1)}, u32[]{:S(2)}) %copy-start) | copy-done | bytes 1228824
  1.9 0.8 constant_dynamic-slice_fusion.w_mine
  2.7 78.6 %shard_map.113 = (bf16[192,2560]{1,0:T(8,128)(2,1)S(1)}, bf16[160,1536]{1,0:T(8,128)(2,1)S(1)}) custom-call(bf16[192,2560]{1,0:T(8,128)(2,1)} %bitcast.12, f32[2560]{0:T(1024)} %gain.1, bf16[160,480]{1,0:T(8,128)(2,1)} %constant_dynamic-slice_fusion.w_mine, bf16[160,2560]{1,0:T(8,128)(2,1)} %bitcast.13, bf16[160,4096]{1,0:T(8,128)(2,1)} %bitcast.11, ...), custom_call_target="tpu_custom_call" | custom-call | tf_op jit(solution)/shard_map/pallas_call | solution.py:518
  81.3 0.9 %copy.14 = bf16[1,192,2560]{2,1,0:T(8,128)(2,1)} copy(bf16[1,192,2560]{2,1,0:T(8,128)(2,1)S(1)} %bitcast.9) | data formatting | bytes 1966080
  82.2 0.8 copy.15
Async XLA Ops:
  0.6 1.3 %copy-start = (bf16[160,3840]{1,0:T(8,128)(2,1)S(1)}, bf16[160,3840]{1,0:T(8,128)(2,1)}, u32[]{:S(2)}) copy-start(bf16[160,3840]{1,0:T(8,128)(2,1)} %param.12) | copy-start | bytes 3686404
